TPU v7x, 32 devices: a whole 2x2x4 slice. The times are simulated.
32 devices in a mesh: rep: 2 (over x), ep: 4 (over y, core), grp: 4 (over z).
Axes of the slice: x: 2, y: 2, z: 4, core: 2. Of those that a mesh axis runs over, the one named last changes fastest.
Arguments:
- tokens: bfloat16 [4096, 4096], P(('rep', 'ep'), 'grp'), parts along dimension 0, may hold values from -6 to 6
- proj_in: bfloat16 [1024, 4096], P('ep', 'grp'), may hold values from -0.09375 to 0.09375
- proj_out: bfloat16 [1024, 4096], P('ep', 'grp'), may hold values from -0.1875 to 0.1875
- expert_up: bfloat16 [16, 1024, 2688], P(('ep', 'grp')), may hold values from -0.1875 to 0.1875
- expert_down: bfloat16 [16, 2688, 1024], P(('ep', 'grp')), may hold values from -0.125 to 0.125
- expert_ids: int32 [4096, 6], P(('rep', 'ep')), parts along dimension 0, may hold values from 0 to 15, as said below
- weight_codes: int32 [4096, 6], P(('rep', 'ep')), parts along dimension 0, may hold values from 1 to 64
Outputs:
- mixed: bfloat16 [4096, 4096], P(('rep', 'ep'), 'grp'), parts along dimension 0
There are 2 independent parts, one for each index of `rep`. A program takes and returns all parts, laid end to end along the dimension named above; an argument that names none is the same for every part. Nothing has to cross between parts.
Inputs may be any that keep to these rules, and one draw needn't show every extreme that they name: `expert_ids`: expert e belongs to group e % 4. Each token picks 6 distinct experts, two in each of 3 distinct groups. Within each aligned block of 128 tokens (the tokens of one device), every group is picked from by exactly 96 tokens, no expert is picked by more than 64 tokens, and in every block each group has an expert picked by exactly 64.
All inputs are finite; a program needn't handle non-finite values.
Results may differ from a plain program's by a relative error of at most 0.012.
Values may be sent and summed in bfloat16 or wider, within the bound.
A program may use at most 64 MiB of HBM per device.

v0:
```python
import functools

import jax
import jax.numpy as jnp
from jax import lax
from jax.experimental import pallas as pl
from jax.experimental.pallas import tpu as pltpu
from jax.sharding import PartitionSpec as P


def expert_block(arrived, expert_up, expert_down):
    width = arrived.shape[-1]
    flat_rows = arrived.reshape(-1, width)
    hidden = jnp.dot(flat_rows, expert_up[0], preferred_element_type=jnp.float32)
    hidden = jnp.square(jnp.maximum(hidden, 0.0)).astype(jnp.bfloat16)
    result = jnp.dot(hidden, expert_down[0], preferred_element_type=jnp.float32)
    return result.astype(jnp.bfloat16).reshape(arrived.shape)


def slot_positions(bucket, live, buckets):
    labels = jnp.arange(buckets, dtype=jnp.int32)
    onehot = jnp.logical_and(bucket[:, :, None] == labels, live[:, :, None]).astype(jnp.int32)
    per_row = jnp.sum(onehot, axis=1)
    before = jnp.cumsum(per_row, axis=0) - per_row
    return jnp.take_along_axis(before, bucket, axis=1)


def per_device(tokens, proj_in, proj_out, expert_up, expert_down, expert_ids, weight_codes):
    ep_count = lax.axis_size("ep")
    group_count = lax.axis_size("grp")
    experts = ep_count * group_count
    tok_block = tokens.shape[0]
    tok_dev = tok_block // group_count
    picks = expert_ids.shape[1]
    width = expert_up.shape[1]
    capacity = max(2, (4 * tok_dev * picks + 3 * experts - 1) // (3 * experts))
    in_rows, out_rows = (
        lax.all_gather(proj_in, "ep", axis=0, tiled=True),
        lax.all_gather(proj_out, "ep", axis=0, tiled=True),
    )
    latent = lax.psum_scatter(
        lax.dot_general(
            tokens, in_rows, (((1,), (1,)), ((), ())), preferred_element_type=jnp.float32
        ),
        "grp",
        scatter_dimension=0,
        tiled=True,
    ).astype(jnp.bfloat16)
    codes = weight_codes.astype(jnp.float32)
    route_weights = codes / jnp.sum(codes, axis=1, keepdims=True)
    group_index = lax.axis_index("grp")
    my_ids = lax.dynamic_slice_in_dim(expert_ids, group_index * tok_dev, tok_dev, 0)
    my_weights = lax.dynamic_slice_in_dim(route_weights, group_index * tok_dev, tok_dev, 0)
    position = slot_positions(my_ids, jnp.ones(my_ids.shape, jnp.bool_), experts)
    spread = jnp.broadcast_to(latent[:, None, :], (tok_dev, picks, width))
    outgoing = jnp.zeros((experts, capacity, width), jnp.bfloat16).at[my_ids, position].set(spread)
    computed = expert_block(
        lax.all_to_all(outgoing, ("ep", "grp"), split_axis=0, concat_axis=0, tiled=True),
        expert_up,
        expert_down,
    )
    returned = lax.all_to_all(computed, ("ep", "grp"), split_axis=0, concat_axis=0, tiled=True)
    picked = returned[my_ids, position]
    combined = jnp.sum(my_weights[:, :, None] * picked.astype(jnp.float32), axis=1)
    latent_out = combined.astype(jnp.bfloat16)
    mixed = jnp.dot(
        lax.all_gather(latent_out, "grp", axis=0, tiled=True),
        out_rows,
        preferred_element_type=jnp.float32,
    )
    return mixed.astype(jnp.bfloat16)


MESH = pl.DeviceIdType.MESH
BF = jnp.bfloat16
F32 = jnp.float32


def nt(a, b):
    return lax.dot_general(a, b, (((1,), (1,)), ((), ())), preferred_element_type=F32)


def nn(a, b):
    return jnp.dot(a, b, preferred_element_type=F32)


def fused_kernel(
    groups, blocks, hits, cap,
    tok, pin, pout, routing, up_hbm, down_hbm, out,
    up, down, win, wout, meta, onehot_t, onehot, inv,
    own, r1, l1, sr1, sl1, lat, xs, xin, hid, ys, mates, zsum, yret, sown, r2, l2, sr2, sl2,
    hbm_sem, ag_s, ag_r, r1s, r1r, l1s, l1r, xss, xsr, ms, mr, yss, ysr, r2s, r2r, l2s, l2r,
):
    ep, z = lax.axis_index("ep"), lax.axis_index("grp")
    chip = ep // 2
    mate = chip * 2 + (1 - ep % 2)
    ypart = (ep + 2) % 4
    rows = tok.shape[0] // blocks
    half = own.shape[2]
    picks = routing.shape[0] // 2
    far = jnp.maximum(z, groups - 1 - z)

    def rcopy(src, dst, s, r, **dev):
        return pltpu.make_async_remote_copy(
            src_ref=src, dst_ref=dst, send_sem=s, recv_sem=r, device_id=dev, device_id_type=MESH
        )

    loads = [
        pltpu.make_async_copy(up_hbm.at[0], up, hbm_sem.at[0]),
        pltpu.make_async_copy(down_hbm.at[0], down, hbm_sem.at[1]),
    ]

    barrier = pltpu.get_barrier_semaphore()
    for peer in (mate, ypart):
        pl.semaphore_signal(barrier, inc=1, device_id={"ep": peer}, device_id_type=MESH)

    @pl.when(z > 0)
    def _():
        pl.semaphore_signal(barrier, inc=1, device_id={"grp": z - 1}, device_id_type=MESH)

    @pl.when(z < groups - 1)
    def _():
        pl.semaphore_signal(barrier, inc=1, device_id={"grp": z + 1}, device_id_type=MESH)

    inner = jnp.logical_and(z > 0, z < groups - 1)
    pl.semaphore_wait(barrier, jnp.where(inner, 4, 3))

    def ag(kind, src, buf, at_own, at_y, mine_y, mine_mate, relay_to):
        to_y = rcopy(src, buf.at[mine_y], ag_s.at[kind, 0], ag_r.at[kind, 0], ep=ypart)
        to_mate = rcopy(src, buf.at[mine_mate], ag_s.at[kind, 1], ag_r.at[kind, 1], ep=mate)
        relay = rcopy(buf.at[at_y], buf.at[relay_to], ag_s.at[kind, 2], ag_r.at[kind, 2], ep=mate)
        return to_y, to_mate, relay

    win_y, win_m, win_relay = ag(0, pin, win, ep, ypart, ep, ep, ypart)
    wout_y, wout_m, wout_relay = ag(1, pout, wout, ep, ypart, ep, ep, ypart)
    meta_y, meta_m, meta_relay = ag(2, meta.at[0], meta, 0, 1, 1, 2, 3)
    win_y.start()
    win_m.start()
    for load in loads:
        load.start()

    ids = routing[0:picks, :]
    codes = routing[picks : 2 * picks, :].astype(F32)
    experts_here = lax.broadcasted_iota(jnp.int32, (8, ids.shape[1]), 0) * groups + z
    table = jnp.zeros((8, ids.shape[1]), F32)
    for p in range(picks):
        table = table + jnp.where(ids[p : p + 1, :] == experts_here, codes[p : p + 1, :], 0.0)
    inverse = 1.0 / jnp.sum(codes, axis=0, keepdims=True)
    hit = jnp.where(jnp.sum(table, axis=0, keepdims=True) > 0.0, 1.0, 0.0)

    def before(n):
        i = lax.broadcasted_iota(jnp.int32, (n, n), 0)
        j = lax.broadcasted_iota(jnp.int32, (n, n), 1)
        return jnp.where(i < j, 1.0, 0.0).astype(BF)

    def ranked(sel, count):
        n = sel.shape[1]
        rank = nn(jnp.broadcast_to(sel, (8, n)).astype(BF), before(n))[0:1, :]
        slot = lax.broadcasted_iota(jnp.int32, (count, n), 0).astype(F32)
        return jnp.where(jnp.logical_and(slot == rank, sel > 0.0), 1.0, 0.0)

    for b in range(blocks):
        at = slice(b * rows, (b + 1) * rows)
        chosen = ranked(hit[:, at], hits)
        onehot[b] = chosen.astype(BF)
        onehot_t[b] = jnp.transpose(chosen).astype(BF)
        meta[0, b] = nt(table[:, at].astype(BF), chosen.astype(BF))
        inv[b] = jnp.transpose(jnp.broadcast_to(inverse[:, at], (rows, rows)))
    meta_y.start()
    meta_m.start()

    win[ep] = pin[...]
    wout[ep] = pout[...]
    win_m.wait_recv()

    def partial(h):
        w = win[pl.ds(2 * jnp.where(h == 0, chip, 1 - chip), 2)].reshape(half, win.shape[2])
        for b in range(blocks):
            own[h * blocks + b] = nt(tok[b * rows : (b + 1) * rows, :], w)

    def hop(k, recv, send, s, r, first, last, dest, mine):
        @pl.when(jnp.logical_not(first))
        def _():
            rcopy(send.at[k], recv.at[k], s.at[k], r.at[k], grp=dest).wait_recv()

        @pl.when(jnp.logical_not(last))
        def _():
            @pl.when(first)
            def _():
                send[k] = mine[k].astype(BF)

            @pl.when(jnp.logical_not(first))
            def _():
                send[k] = (mine[k].astype(F32) + recv[k].astype(F32)).astype(BF)

            rcopy(send.at[k], recv.at[k], s.at[k], r.at[k], grp=dest).start()

    right = jnp.minimum(z + 1, groups - 1)
    left = jnp.maximum(z - 1, 0)

    def hops(t, n, bufs, mine):
        rr, ll, ss, sl, rs_, rr_, ls_, lr_ = bufs
        kr, kl = t - z, t - (groups - 1 - z)

        @pl.when(jnp.logical_and(kr >= 0, kr < n))
        def _():
            hop(kr, rr, ss, rs_, rr_, z == 0, z == groups - 1, right, mine)

        @pl.when(jnp.logical_and(kl >= 0, kl < n))
        def _():
            hop(kl, ll, sl, ls_, lr_, z == groups - 1, z == 0, left, mine)

    def total(k, rr, ll, mine, finish):
        @pl.when(z == 0)
        def _():
            finish(mine[k].astype(F32) + ll[k].astype(F32))

        @pl.when(z == groups - 1)
        def _():
            finish(mine[k].astype(F32) + rr[k].astype(F32))

        @pl.when(jnp.logical_and(z > 0, z < groups - 1))
        def _():
            finish(mine[k].astype(F32) + rr[k].astype(F32) + ll[k].astype(F32))

    def x_copies(b):
        return (
            rcopy(xs.at[b, 0], xs.at[b, 1], xss.at[b, 0], xsr.at[b, 0], ep=ypart),
            rcopy(xs.at[b, 0], xs.at[b, 2], xss.at[b, 1], xsr.at[b, 1], ep=mate),
            rcopy(xs.at[b, 1], xs.at[b, 3], xss.at[b, 2], xsr.at[b, 2], ep=mate),
        )

    bufs1 = (r1, l1, sr1, sl1, r1s, r1r, l1s, l1r)
    chunks = 2 * blocks

    def step1(t, _):
        hops(t, chunks, bufs1, own)
        k = t - far

        @pl.when(jnp.logical_and(k >= 0, k < chunks))
        def _():
            h = k // blocks
            b = k % blocks
            column = pl.multiple_of(jnp.where(h == 0, chip, 1 - chip) * half, half)

            def finish(v):
                lat[b, :, pl.ds(column, half)] = v.astype(BF)

            total(k, r1, l1, own, finish)

            @pl.when(h == 1)
            def _():
                xs[b, 0] = nn(onehot[b], lat[b]).astype(BF)
                a, c, _ = x_copies(b)
                a.start()
                c.start()

        return 0

    partial(0)
    lax.fori_loop(0, blocks, step1, 0)
    win_y.wait_recv()
    win_relay.start()
    meta_y.wait_recv()
    meta_relay.start()
    wout_m.start()
    wout_y.start()
    win_relay.wait_recv()
    partial(1)
    lax.fori_loop(blocks, chunks + groups - 1, step1, 0)
    for load in loads:
        load.wait()
    meta_m.wait_recv()
    meta_relay.wait_recv()

    def m_copy(b):
        return rcopy(ys.at[b, pl.ds(2, 2)], mates.at[b], ms.at[b], mr.at[b], ep=mate)

    def y_copy(b):
        return rcopy(zsum.at[b, 1], yret.at[b], yss.at[b], ysr.at[b], ep=ypart)

    bufs2 = (r2, l2, sr2, sl2, r2s, r2r, l2s, l2r)

    def step2(u, _):
        @pl.when(u < blocks)
        def _():
            b = u
            a, c, relay = x_copies(b)
            a.wait_recv()
            relay.start()
            c.wait_recv()
            relay.wait_recv()
            scaled = []
            for s in range(4):
                m = meta[s, b, pl.ds(ep, 1), :]
                q = ranked(jnp.where(m > 0.0, 1.0, 0.0), cap)
                xin[s * cap : (s + 1) * cap, :] = nn(q.astype(BF), xs[b, s]).astype(BF)
                scaled.append(jnp.transpose(q * m).astype(BF))
            h = jnp.maximum(nn(xin[...], up[...]), 0.0)
            hid[...] = (h * h).astype(BF)
            o = nn(hid[...], down[...]).astype(BF)
            for s in range(4):
                ys[b, s] = nn(scaled[s], o[s * cap : (s + 1) * cap, :]).astype(BF)
            m_copy(b).start()

        @pl.when(jnp.logical_and(u >= 1, u < blocks + 1))
        def _():
            b = u - 1
            m_copy(b).wait_recv()
            zsum[b] = (ys[b, 0:2].astype(F32) + mates[b].astype(F32)).astype(BF)
            y_copy(b).start()

        @pl.when(u == 1)
        def _():
            wout_y.wait_recv()
            wout_relay.start()

        @pl.when(jnp.logical_and(u >= 2, u < blocks + 2))
        def _():
            b = u - 2
            y_copy(b).wait_recv()
            v = (zsum[b, 0].astype(F32) + yret[b].astype(F32)).astype(BF)
            sown[b] = nn(onehot_t[b], v).astype(BF)

        @pl.when(u == 3)
        def _():
            wout_m.wait_recv()
            wout_relay.wait_recv()

        t = u - 2
        hops(t, blocks, bufs2, sown)
        k = t - far

        @pl.when(jnp.logical_and(k >= 0, k < blocks))
        def _():
            def finish(v):
                w = jnp.concatenate([inv[k]] * (v.shape[1] // rows), axis=1)
                y = (v * w).astype(BF)
                full = wout[...].reshape(v.shape[1], wout.shape[2])
                out[pl.ds(pl.multiple_of(k * rows, rows), rows), :] = nn(y, full).astype(BF)

            total(k, r2, l2, sown, finish)

        return 0

    lax.fori_loop(0, blocks + 2 + groups - 1, step2, 0)

    for copy in (win_y, win_m, win_relay, wout_y, wout_m, wout_relay, meta_y, meta_m, meta_relay):
        copy.wait_send()

    def drain(n, bufs):
        rr, ll, ss, sl, rs_, rr_, ls_, lr_ = bufs

        @pl.when(z < groups - 1)
        def _():
            for k in range(n):
                rcopy(ss.at[k], rr.at[k], rs_.at[k], rr_.at[k], grp=right).wait_send()

        @pl.when(z > 0)
        def _():
            for k in range(n):
                rcopy(sl.at[k], ll.at[k], ls_.at[k], lr_.at[k], grp=left).wait_send()

    drain(chunks, bufs1)
    drain(blocks, bufs2)
    for b in range(blocks):
        for copy in x_copies(b):
            copy.wait_send()
        m_copy(b).wait_send()
        y_copy(b).wait_send()


def fused_device(sizes, tokens, proj_in, proj_out, expert_up, expert_down, expert_ids, weight_codes):
    groups = sizes["grp"]
    blocks = groups
    rows = tokens.shape[0] // blocks
    picks = expert_ids.shape[1]
    experts = sizes["ep"] * groups
    hits = rows * (picks // 2) // groups
    cap = max(2, (4 * rows * picks + 3 * experts - 1) // (3 * experts))
    latent, features = proj_in.shape[0] * sizes["ep"], proj_in.shape[1]
    hidden = expert_up.shape[2]
    half = latent // 2
    routing = jnp.concatenate([expert_ids.T, weight_codes.T], axis=0)
    chunks = 2 * blocks
    vm = pltpu.VMEM
    dma = pltpu.SemaphoreType.DMA
    scratch = [
        vm((latent, hidden), BF), vm((hidden, latent), BF),
        vm((4, *proj_in.shape), BF), vm((4, *proj_out.shape), BF),
        vm((4, blocks, 8, hits), F32), vm((blocks, rows, hits), BF), vm((blocks, hits, rows), BF),
        vm((blocks, rows, rows), F32),
        vm((chunks, rows, half), F32),
        *[vm((chunks, rows, half), BF)] * 4,
        vm((blocks, rows, latent), BF),
        vm((blocks, 4, hits, latent), BF),
        vm((4 * cap, latent), BF), vm((4 * cap, hidden), BF),
        vm((blocks, 4, hits, latent), BF),
        vm((blocks, 2, hits, latent), BF), vm((blocks, 2, hits, latent), BF),
        vm((blocks, hits, latent), BF),
        vm((blocks, rows, latent), BF),
        *[vm((blocks, rows, latent), BF)] * 4,
        dma((2,)), dma((3, 3)), dma((3, 3)),
        *[dma((chunks,))] * 4,
        dma((blocks, 3)), dma((blocks, 3)),
        *[dma((blocks,))] * 8,
    ]
    vmem = pl.BlockSpec(memory_space=pltpu.VMEM)
    hbm = pl.BlockSpec(memory_space=pl.ANY)
    return pl.pallas_call(
        functools.partial(fused_kernel, groups, blocks, hits, cap),
        out_shape=jax.ShapeDtypeStruct((tokens.shape[0], features), BF),
        in_specs=[vmem, vmem, vmem, vmem, hbm, hbm],
        out_specs=vmem,
        scratch_shapes=scratch,
        compiler_params=pltpu.CompilerParams(
            collective_id=0, has_side_effects=True, vmem_limit_bytes=60 << 20
        ),
    )(tokens, proj_in, proj_out, routing, expert_up, expert_down)


def solution(mesh):
    sizes = dict(mesh.shape)
    body = per_device
    if sizes["ep"] == 4 and sizes["grp"] <= 4:
        body = functools.partial(fused_device, sizes)
    in_specs = (
        P(("rep", "ep"), "grp"),
        P("ep", "grp"),
        P("ep", "grp"),
        P(("ep", "grp"), None, None),
        P(("ep", "grp"), None, None),
        P(("rep", "ep"), None),
        P(("rep", "ep"), None),
    )
    out_specs = P(("rep", "ep"), "grp")
    return jax.shard_map(
        body, mesh=mesh, in_specs=in_specs, out_specs=out_specs, check_vma=False
    )
```

profile of v0, /device:TPU:0, one launch (start us, length us, event | category | flops | bytes accessed | tf_op | source)
XLA Modules:
  0.0 120.3 jit_solution(12767269831147531446)
XLA Ops:
  0.0 1.4 %pad_add_fusion.routing = s32[12,512]{1,0:T(8,128)} fusion(s32[6,512]{1,0:T(8,128)} %bitcast.2, s32[6,512]{1,0:T(8,128)} %bitcast.3), kind=kLoop, calls=%fused_computation | loop fusion | flops 6144 | bytes 49152 | tf_op jit(solution)/shard_map/concatenate | solution.py:384
  1.4 116.7 %shard_map.73 = bf16[512,1024]{1,0:T(8,128)(2,1)} custom-call(bf16[512,1024]{1,0:T(8,128)(2,1)} %tok.1, bf16[256,1024]{1,0:T(8,128)(2,1)} %pin.1, bf16[256,1024]{1,0:T(8,128)(2,1)} %pout.1, s32[12,512]{1,0:T(8,128)} %pad_add_fusion.routing, bf16[1,1024,2688]{2,1,0:T(8,128)(2,1)} %up_hbm.1, bf16[1,2688,1024]{2,1,0:T(8,128)(2,1)} %down_hbm.1), custom_call_target="tpu_custom_call" | custom-call | tf_op jit(solution)/shard_map/pallas_call | solution.py:410
  118.1 2.3 %copy.9 = bf16[512,1024]{1,0:T(8,128)(2,1)} copy(bf16[512,1024]{1,0:T(8,128)(2,1)} %shard_map.73) | data formatting | bytes 2097152
where the time goes:
time: 121 us; the launch traced here: 120 us
  Pallas kernels  117 us (97%)
  local copies, waits for them, and re-layouts  2.26 us (2%)
  other arithmetic  1.36 us (1%)
    pallas_call x1, Pallas kernels, fused_device(): pl.pallas_call(functools.partial(fused_kernel, groups, blocks, hits, cap)...  117 us

commit v1 on v0

v1 whole, which is shorter than its diff:
```python
import functools

import jax
import jax.numpy as jnp
from jax import lax
from jax.experimental import pallas as pl
from jax.experimental.pallas import tpu as pltpu
from jax.sharding import PartitionSpec as P


def expert_block(arrived, expert_up, expert_down):
    width = arrived.shape[-1]
    flat_rows = arrived.reshape(-1, width)
    hidden = jnp.dot(flat_rows, expert_up[0], preferred_element_type=jnp.float32)
    hidden = jnp.square(jnp.maximum(hidden, 0.0)).astype(jnp.bfloat16)
    result = jnp.dot(hidden, expert_down[0], preferred_element_type=jnp.float32)
    return result.astype(jnp.bfloat16).reshape(arrived.shape)


def slot_positions(bucket, live, buckets):
    labels = jnp.arange(buckets, dtype=jnp.int32)
    onehot = jnp.logical_and(bucket[:, :, None] == labels, live[:, :, None]).astype(jnp.int32)
    per_row = jnp.sum(onehot, axis=1)
    before = jnp.cumsum(per_row, axis=0) - per_row
    return jnp.take_along_axis(before, bucket, axis=1)


def per_device(tokens, proj_in, proj_out, expert_up, expert_down, expert_ids, weight_codes):
    ep_count = lax.axis_size("ep")
    group_count = lax.axis_size("grp")
    experts = ep_count * group_count
    tok_block = tokens.shape[0]
    tok_dev = tok_block // group_count
    picks = expert_ids.shape[1]
    width = expert_up.shape[1]
    capacity = max(2, (4 * tok_dev * picks + 3 * experts - 1) // (3 * experts))
    in_rows, out_rows = (
        lax.all_gather(proj_in, "ep", axis=0, tiled=True),
        lax.all_gather(proj_out, "ep", axis=0, tiled=True),
    )
    latent = lax.psum_scatter(
        lax.dot_general(
            tokens, in_rows, (((1,), (1,)), ((), ())), preferred_element_type=jnp.float32
        ),
        "grp",
        scatter_dimension=0,
        tiled=True,
    ).astype(jnp.bfloat16)
    codes = weight_codes.astype(jnp.float32)
    route_weights = codes / jnp.sum(codes, axis=1, keepdims=True)
    group_index = lax.axis_index("grp")
    my_ids = lax.dynamic_slice_in_dim(expert_ids, group_index * tok_dev, tok_dev, 0)
    my_weights = lax.dynamic_slice_in_dim(route_weights, group_index * tok_dev, tok_dev, 0)
    position = slot_positions(my_ids, jnp.ones(my_ids.shape, jnp.bool_), experts)
    spread = jnp.broadcast_to(latent[:, None, :], (tok_dev, picks, width))
    outgoing = jnp.zeros((experts, capacity, width), jnp.bfloat16).at[my_ids, position].set(spread)
    computed = expert_block(
        lax.all_to_all(outgoing, ("ep", "grp"), split_axis=0, concat_axis=0, tiled=True),
        expert_up,
        expert_down,
    )
    returned = lax.all_to_all(computed, ("ep", "grp"), split_axis=0, concat_axis=0, tiled=True)
    picked = returned[my_ids, position]
    combined = jnp.sum(my_weights[:, :, None] * picked.astype(jnp.float32), axis=1)
    latent_out = combined.astype(jnp.bfloat16)
    mixed = jnp.dot(
        lax.all_gather(latent_out, "grp", axis=0, tiled=True),
        out_rows,
        preferred_element_type=jnp.float32,
    )
    return mixed.astype(jnp.bfloat16)


MESH = pl.DeviceIdType.MESH
BF = jnp.bfloat16
F32 = jnp.float32


def nt(a, b):
    return lax.dot_general(a, b, (((1,), (1,)), ((), ())), preferred_element_type=F32)


def nn(a, b):
    return jnp.dot(a, b, preferred_element_type=F32)


SHARED = ("E1", "E2", "E3", "META", "O", "P", "Q")
OUTER = (
    ("P", 0), ("META",), ("P", 1), ("GWX", 0), ("WOUT",), ("GWX", 1), ("METAR",), ("T", 0), ("GWM", 0),
    ("Q", 0), ("Q", 1), ("T", 1), ("Q", 2), ("Q", 3), ("T", 2), ("GWM", 1), ("P", 2), ("P", 3), ("T", 3),
    ("WX",), ("T", 4), ("D", 0, 0), ("T", 5), ("D", 1, 0), ("T", 6), ("D", 2, 0), ("R", 0, 0), ("T", 7),
    ("D", 3, 0), ("WR",), ("R", 1, 0), ("T", 8), ("T", 9), ("R", 2, 0), ("T", 10), ("D", 0, 1), ("R", 3, 0),
    ("T", 11), ("D", 1, 1), ("T", 12), ("R", 0, 1), ("T", 13), ("D", 2, 1), ("E1", 0), ("T", 14), ("R", 1,
    1), ("E2", 0), ("E3", 0, 0), ("T", 15), ("D", 3, 1), ("R", 2, 1), ("E3", 0, 1), ("M", 0, 0), ("E1", 1),
    ("M", 0, 1), ("E2", 1), ("R", 3, 1), ("E3", 1, 0), ("E3", 1, 1), ("Y", 0, 0), ("M", 1, 0), ("E1", 2),
    ("M", 1, 1), ("Y", 0, 1), ("E2", 2), ("E3", 2, 0), ("Y", 1, 0), ("E3", 2, 1), ("M", 2, 0), ("Y", 1, 1),
    ("E1", 3), ("M", 2, 1), ("E2", 3), ("H", 0, 0), ("E3", 3, 0), ("H", 0, 1), ("Y", 2, 0), ("E3", 3, 1),
    ("H", 0, 2), ("M", 3, 0), ("Y", 2, 1), ("M", 3, 1), ("H", 0, 3), ("O", 0), ("H", 1, 0), ("Y", 3, 0),
    ("H", 1, 1), ("Y", 3, 1), ("H", 1, 2), ("H", 1, 3), ("O", 1), ("H", 2, 0), ("H", 2, 1), ("H", 2, 2),
    ("H", 2, 3), ("O", 2), ("H", 3, 0), ("H", 3, 1), ("H", 3, 2), ("H", 3, 3), ("O", 3),
)
INNER = (
    ("P", 0), ("META",), ("P", 1), ("F1", 0), ("GWX", 0), ("F1", 1), ("WOUT",), ("F2", 0), ("F1", 2), ("F2",
    1), ("GWX", 1), ("F1", 3), ("METAR",), ("GWM", 0), ("F2", 2), ("F1", 4), ("Q", 0), ("Q", 1), ("F2", 3),
    ("F1", 5), ("Q", 2), ("Q", 3), ("GWM", 1), ("F1", 6), ("F2", 4), ("D", 0, 0), ("P", 2), ("P", 3), ("F1",
    7), ("F2", 5), ("D", 1, 0), ("WX",), ("F2", 6), ("F1", 8), ("D", 2, 0), ("R", 0, 0), ("F1", 9), ("F2",
    7), ("D", 3, 0), ("F1", 10), ("F2", 8), ("R", 1, 0), ("F1", 11), ("F2", 9), ("R", 2, 0), ("F1", 12),
    ("F2", 10), ("D", 0, 1), ("WR",), ("F1", 13), ("F2", 11), ("D", 1, 1), ("R", 3, 0), ("F1", 14), ("F2",
    12), ("R", 0, 1), ("F1", 15), ("F2", 13), ("D", 2, 1), ("E1", 0), ("F2", 14), ("R", 1, 1), ("E2", 0),
    ("F2", 15), ("D", 3, 1), ("E3", 0, 0), ("R", 2, 1), ("E3", 0, 1), ("E1", 1), ("R", 3, 1), ("M", 0, 0),
    ("M", 0, 1), ("E2", 1), ("E3", 1, 0), ("E3", 1, 1), ("Y", 0, 0), ("M", 1, 0), ("E1", 2), ("M", 1, 1),
    ("Y", 0, 1), ("E2", 2), ("E3", 2, 0), ("Y", 1, 0), ("E3", 2, 1), ("G1", 0, 0), ("M", 2, 0), ("Y", 1, 1),
    ("G1", 0, 1), ("E1", 3), ("G1", 0, 2), ("M", 2, 1), ("G2", 0, 0), ("E2", 3), ("G1", 0, 3), ("Y", 2, 0),
    ("G2", 0, 1), ("E3", 3, 0), ("G1", 1, 0), ("G2", 0, 2), ("Y", 2, 1), ("G1", 1, 1), ("E3", 3, 1), ("G1",
    1, 2), ("G2", 0, 3), ("M", 3, 0), ("G2", 1, 0), ("O", 0), ("G1", 1, 3), ("M", 3, 1), ("G2", 1, 1),
    ("G1", 2, 0), ("G2", 1, 2), ("Y", 3, 0), ("G1", 2, 1), ("G2", 1, 3), ("O", 1), ("G1", 2, 2), ("Y", 3,
    1), ("G2", 2, 0), ("G1", 2, 3), ("G2", 2, 1), ("G1", 3, 0), ("G2", 2, 2), ("G1", 3, 1), ("G2", 2, 3),
    ("O", 2), ("G1", 3, 2), ("G2", 3, 0), ("G1", 3, 3), ("G2", 3, 1), ("G2", 3, 2), ("G2", 3, 3), ("O", 3),
)
CHUNKS = ((0, 0), (0, 1), (0, 2), (0, 3), (1, 0), (1, 1), (1, 2), (1, 3), (2, 0), (2, 1), (3, 0), (3, 1), (2, 2), (3, 2), (2, 3), (3, 3))


def segments():
    def cut(steps):
        parts = [[]]
        for step in steps:
            if step[0] in SHARED:
                parts[-1].append(step)
                parts.append([])
            else:
                parts[-1].append(step)
        return parts

    return list(zip(cut(OUTER), cut(INNER)))


def fused_kernel(
    blocks, hits, cap,
    tok, ids, codes, pin, pout, up_hbm, down_hbm, out,
    up, down, win, wout, meta, onehot_t, onehot, inv, pick, scale,
    own, s1, s2, f1, f2, lat, xs, xin, hid, ys, mates, zsum, yret, sown, s3, s4, f3, f4, ybuf,
    hbm_sem, ws, wr, os_, or_, mts, mtr, ai, bo, ra, rb, xss, xsr, ms, mr, yss, ysr, ci, co, rc, rd,
):
    rep, ep, z = lax.axis_index("rep"), lax.axis_index("ep"), lax.axis_index("grp")
    chip = ep // 2
    side = ep % 2
    mate = chip * 2 + (1 - side)
    ypart = (ep + 2) % 4
    inward = jnp.where(z < 2, z + 1, z - 1)
    outward = jnp.where(z < 2, jnp.maximum(z - 1, 0), jnp.minimum(z + 1, 3))
    inner = jnp.logical_and(z > 0, z < 3)
    outer = jnp.logical_not(inner)
    rows = tok.shape[0] // blocks
    quarter = pin.shape[0]
    half = 2 * quarter
    picks = ids.shape[1]
    pieces = ws.shape[0] // 4
    prow = quarter // 2 // pieces
    split = sown.shape[1]
    width = sown.shape[3]

    def rcopy(src, dst, s, r, **dev):
        return pltpu.make_async_remote_copy(
            src_ref=src, dst_ref=dst, send_sem=s, recv_sem=r, device_id=dev, device_id_type=MESH
        )

    loads = [
        pltpu.make_async_copy(up_hbm.at[0], up, hbm_sem.at[0]),
        pltpu.make_async_copy(down_hbm.at[0], down, hbm_sem.at[1]),
    ]

    barrier = pltpu.get_barrier_semaphore()
    for dev in ({"ep": mate}, {"ep": ypart}, {"rep": 1 - rep}, {"grp": inward}):
        pl.semaphore_signal(barrier, inc=1, device_id=dev, device_id_type=MESH)

    @pl.when(inner)
    def _():
        pl.semaphore_signal(barrier, inc=1, device_id={"grp": outward}, device_id_type=MESH)

    def gather(src, buf, at_mate, at_y, n, s, r):
        def part(which, p):
            return pl.ds(pl.multiple_of(which * (n * step) + p * step, step), step)

        step = src.shape[0] // 2 // n
        to_y, to_x, on_y, on_x = [], [], [], []
        src_slot, y_src, y_slot, relay_slot = at_mate[0], at_y[0], at_y[1], at_mate[1]
        for p in range(n):
            mine, other = part(rep, p), part(1 - rep, p)
            to_y.append(rcopy(src.at[mine], buf.at[y_src, mine], s.at[4 * p], r.at[4 * p], ep=ypart))
            to_x.append(
                rcopy(buf.at[y_slot, mine], buf.at[y_slot, mine], s.at[4 * p + 1], r.at[4 * p + 1], rep=1 - rep)
            )
            on_y.append(
                rcopy(buf.at[y_slot, mine], buf.at[relay_slot, mine], s.at[4 * p + 2], r.at[4 * p + 2], ep=mate)
            )
            on_x.append(
                rcopy(buf.at[y_slot, other], buf.at[relay_slot, other], s.at[4 * p + 3], r.at[4 * p + 3], ep=mate)
            )
        to_mate = rcopy(src, buf.at[src_slot], s.at[4 * n], r.at[4 * n], ep=mate)
        return to_mate, to_y, to_x, on_y, on_x

    win_m, win_y, win_x, win_ry, win_rx = gather(pin, win, (0, 2), (1, 1), pieces, ws, wr)
    out_m, out_y, out_x, out_ry, out_rx = gather(pout, wout, (ep, ypart), (ep, ypart), 1, os_, or_)
    meta_y = rcopy(meta.at[0], meta.at[1], mts.at[0], mtr.at[0], ep=ypart)
    meta_m = rcopy(meta.at[0], meta.at[2], mts.at[1], mtr.at[1], ep=mate)
    meta_r = rcopy(meta.at[1], meta.at[3], mts.at[2], mtr.at[2], ep=mate)

    def from_outer(k):
        return rcopy(s1.at[k], f1.at[k], ai.at[k], ra.at[k], grp=inward)

    def across(k):
        return rcopy(s1.at[k], f2.at[k], ai.at[k], rb.at[k], grp=inward)

    def to_outer(k):
        return rcopy(s2.at[k], f2.at[k], bo.at[k], rb.at[k], grp=outward)

    def keep(q, v):
        for b in range(blocks):
            own[q * blocks + b] = v[b * rows : (b + 1) * rows, :]

        @pl.when(outer)
        def _():
            for b in range(blocks):
                s1[q * blocks + b] = v[b * rows : (b + 1) * rows, :].astype(BF)

    def send_own(q):
        if q < 2:
            ready = [(q, b) for b in range(blocks)]
        else:
            ready = CHUNKS[2 * blocks :][:2] if q == 2 else CHUNKS[2 * blocks + 2 :]

        @pl.when(outer)
        def _():
            for c, b in ready:
                from_outer(c * blocks + b).start()

    def partial(q):
        w = pin[...] if q == 0 else win[q - 1]
        keep(q, nt(tok[...], w))

    for load in loads:
        load.start()
    partial(0)
    pl.semaphore_wait(barrier, jnp.where(inner, 5, 4))
    for copy in (win_m, *win_y):
        copy.start()
    send_own(0)

    def put(q, b, v):
        column = pl.multiple_of(jnp.where(q % 2 == 0, side, 1 - side) * quarter, quarter)
        lat[b, jnp.where(q < 2, chip, 1 - chip), :, pl.ds(column, quarter)] = v.astype(BF)

    def op_f1(k):
        from_outer(k).wait_recv()
        s1[k] = (own[k] + f1[k].astype(F32)).astype(BF)
        across(k).start()

    def op_f2(q, b):
        k = q * blocks + b
        across(k).wait_recv()
        v = own[k] + f2[k].astype(F32)
        s2[k] = v.astype(BF)
        to_outer(k).start()
        put(q, b, v + f1[k].astype(F32))

    def op_t(q, b):
        k = q * blocks + b
        to_outer(k).wait_recv()
        put(q, b, own[k] + f2[k].astype(F32))

    def before(n):
        i = lax.broadcasted_iota(jnp.int32, (n, n), 0)
        j = lax.broadcasted_iota(jnp.int32, (n, n), 1)
        return jnp.where(i < j, 1.0, 0.0).astype(BF)

    def placed(sel, rank, count):
        slot = lax.broadcasted_iota(jnp.int32, (count, sel.shape[1]), 0).astype(F32)
        return jnp.where(jnp.logical_and(slot == rank, sel > 0.0), 1.0, 0.0)

    def op_meta():
        i = lax.broadcasted_iota(jnp.int32, (8, picks), 0)
        j = lax.broadcasted_iota(jnp.int32, (8, picks), 1)
        pickrow = jnp.where(i == j, 1.0, 0.0).astype(BF)
        id_rows = nt(pickrow, ids[...].astype(F32).astype(BF))
        code_rows = nt(pickrow, codes[...].astype(F32).astype(BF))
        n = id_rows.shape[1]
        here = (lax.broadcasted_iota(jnp.int32, (8, n), 0) * blocks + z).astype(F32)
        table = jnp.zeros((8, n), F32)
        for p in range(picks):
            table = table + jnp.where(id_rows[p : p + 1, :] == here, code_rows[p : p + 1, :], 0.0)
        inverse = 1.0 / jnp.sum(code_rows, axis=0, keepdims=True)
        hit = jnp.where(jnp.sum(table, axis=0, keepdims=True) > 0.0, 1.0, 0.0)
        for b in range(blocks):
            at = slice(b * rows, (b + 1) * rows)
            sel = hit[:, at]
            rank = nn(jnp.broadcast_to(sel, (8, rows)).astype(BF), before(rows))[0:1, :]
            chosen = placed(sel, rank, hits)
            onehot[b] = chosen.astype(BF)
            onehot_t[b] = jnp.transpose(chosen).astype(BF)
            meta[0, b] = nt(table[:, at].astype(BF), chosen.astype(BF))
            inv[b] = jnp.transpose(jnp.broadcast_to(inverse[:, at], (rows, rows)))
        meta_y.start()
        meta_m.start()

    def op_metar():
        meta_y.wait_recv()
        meta_r.start()

    def op_q(b):
        if b == 0:
            meta_m.wait_recv()
            meta_r.wait_recv()
        for s in range(4):
            m = meta[s, b, pl.ds(ep, 1), :]
            sel = jnp.where(m > 0.0, 1.0, 0.0)
            rank = nn(jnp.broadcast_to(sel, (8, hits)).astype(BF), before(hits))[0:1, :]
            q = placed(sel, rank, cap)
            pick[b, s] = q.astype(BF)
            scale[b, s] = jnp.transpose(q * m).astype(BF)

    def x_copies(b, g):
        mine = jnp.where(g == 0, chip, 1 - chip)
        other = 1 - mine
        k = 2 * b + g
        return (
            rcopy(xs.at[b, 0, mine], xs.at[b, 1, mine], xss.at[k, 0], xsr.at[k, 0], ep=ypart),
            rcopy(xs.at[b, 0, mine], xs.at[b, 2, mine], xss.at[k, 1], xsr.at[k, 1], ep=mate),
            rcopy(xs.at[b, 1, other], xs.at[b, 3, other], xss.at[k, 2], xsr.at[k, 2], ep=mate),
        )

    def op_d(b, g):
        mine = jnp.where(g == 0, chip, 1 - chip)
        xs[b, 0, mine] = nn(onehot[b], lat[b, mine]).astype(BF)
        to_y, to_m, _ = x_copies(b, g)
        to_y.start()
        to_m.start()

    def op_r(b, g):
        to_y, _, relay = x_copies(b, g)
        to_y.wait_recv()
        relay.start()

    def op_w(b):
        for g in range(2):
            _, to_m, relay = x_copies(b, g)
            to_m.wait_recv()
            relay.wait_recv()

    cut = (hid.shape[1] // 2) // 256 * 256

    def raised(c):
        h = jnp.maximum(nn(xin[...], up[:, c]), 0.0)
        hid[:, c] = (h * h).astype(BF)

    def op_e1(b):
        op_w(b)
        if b == 0:
            for load in loads:
                load.wait()
        for s in range(4):
            for h in range(2):
                xin[s * cap : (s + 1) * cap, h * half : (h + 1) * half] = nn(
                    pick[b, s], xs[b, s, h]
                ).astype(BF)
        raised(slice(0, cut))

    def op_e2(b):
        raised(slice(cut, hid.shape[1]))

    def m_copy(b, h):
        return rcopy(ys.at[b, h, pl.ds(2, 2)], mates.at[b, h], ms.at[b, h], mr.at[b, h], ep=mate)

    def y_copy(b, h):
        return rcopy(zsum.at[b, h, 1], yret.at[b, h], yss.at[b, h], ysr.at[b, h], ep=ypart)

    def op_e3(b, h):
        o = nn(hid[...], down[:, h * half : (h + 1) * half]).astype(BF)
        for s in (2, 3, 0, 1):
            ys[b, h, s] = nn(scale[b, s], o[s * cap : (s + 1) * cap, :]).astype(BF)
        m_copy(b, h).start()

    def op_m(b, h):
        m_copy(b, h).wait_recv()
        zsum[b, h] = (ys[b, h, 0:2].astype(F32) + mates[b, h].astype(F32)).astype(BF)
        y_copy(b, h).start()

    def from_outer2(b, c):
        return rcopy(sown.at[b, c], f3.at[b, c], ci.at[b, c], rc.at[b, c], grp=inward)

    def across2(b, c):
        return rcopy(s3.at[b, c], f4.at[b, c], ci.at[b, c], rd.at[b, c], grp=inward)

    def to_outer2(b, c):
        return rcopy(s4.at[b, c], f4.at[b, c], co.at[b, c], rd.at[b, c], grp=outward)

    per_half = split // 2

    def op_y(b, h):
        y_copy(b, h).wait_recv()
        v = (zsum[b, h, 0].astype(F32) + yret[b, h].astype(F32)).astype(BF)
        v = nn(onehot_t[b], v).astype(BF)
        for i in range(per_half):
            sown[b, h * per_half + i] = v[:, i * width : (i + 1) * width]

        @pl.when(outer)
        def _():
            for i in range(per_half):
                from_outer2(b, h * per_half + i).start()

    def op_g1(b, c):
        from_outer2(b, c).wait_recv()
        s3[b, c] = (sown[b, c].astype(F32) + f3[b, c].astype(F32)).astype(BF)
        across2(b, c).start()

    def weigh(b, c, v):
        w = jnp.concatenate([inv[b]] * (width // rows), axis=1)
        ybuf[b, :, c * width : (c + 1) * width] = (v * w).astype(BF)

    def op_g2(b, c):
        across2(b, c).wait_recv()
        v = sown[b, c].astype(F32) + f4[b, c].astype(F32)
        s4[b, c] = v.astype(BF)
        to_outer2(b, c).start()
        weigh(b, c, v + f3[b, c].astype(F32))

    def op_h(b, c):
        to_outer2(b, c).wait_recv()
        weigh(b, c, sown[b, c].astype(F32) + f4[b, c].astype(F32))

    def op_o(b):
        if b == 0:
            out_m.wait_recv()
            out_ry[0].wait_recv()
            out_rx[0].wait_recv()
        full = wout[...].reshape(4 * quarter, wout.shape[2])
        out[b * rows : (b + 1) * rows, :] = nn(ybuf[b], full).astype(BF)

    def op_gwx(p):
        win_y[p].wait_recv()
        win_x[p].start()
        win_ry[p].start()

    def op_gwm(p):
        win_x[p].wait_recv()
        win_rx[p].start()

    def op_p(q):
        if q == 1:
            win_m.wait_recv()
        if q == 3:
            for p in range(pieces):
                win_ry[p].wait_recv()
                win_rx[p].wait_recv()
        partial(q)
        send_own(q)

    def op_wout():
        out_m.start()
        out_y[0].start()
        wout[ep] = pout[...]

    def op_wx():
        out_y[0].wait_recv()
        out_x[0].start()
        out_ry[0].start()

    def op_wr():
        out_x[0].wait_recv()
        out_rx[0].start()

    ops = dict(
        META=op_meta, METAR=op_metar, Q=op_q, P=op_p, D=op_d, R=op_r,
        E1=op_e1, E2=op_e2, E3=op_e3, M=op_m, Y=op_y, G1=op_g1, G2=op_g2, H=op_h, O=op_o,
        GWX=op_gwx, GWM=op_gwm, WOUT=op_wout, WX=op_wx, WR=op_wr,
        F1=lambda j: op_f1(CHUNKS[j][0] * blocks + CHUNKS[j][1]),
        F2=lambda j: op_f2(*CHUNKS[j]), T=lambda j: op_t(*CHUNKS[j]),
    )

    def steps_of(which, steps):
        if steps:
            @pl.when(which)
            def _():
                for name, *args in steps:
                    ops[name](*args)

    for at_outer, at_inner in segments():
        shared = [at_outer.pop(), at_inner.pop()] if at_outer and at_outer[-1][0] in SHARED else None
        steps_of(outer, at_outer)
        steps_of(inner, at_inner)
        if shared and shared[0] != ("P", 0):
            ops[shared[0][0]](*shared[0][1:])

    for copy in (win_m, *win_y, *win_x, *win_ry, *win_rx, out_m, *out_y, *out_x, *out_ry, *out_rx):
        copy.wait_send()
    for copy in (meta_y, meta_m, meta_r):
        copy.wait_send()
    for k in range(4 * blocks):
        from_outer(k).wait_send()
    for b in range(blocks):
        for h in range(2):
            for copy in x_copies(b, h):
                copy.wait_send()
            m_copy(b, h).wait_send()
            y_copy(b, h).wait_send()
        for c in range(split):
            from_outer2(b, c).wait_send()

    @pl.when(inner)
    def _():
        for k in range(4 * blocks):
            to_outer(k).wait_send()
        for b in range(blocks):
            for c in range(split):
                to_outer2(b, c).wait_send()


def fused_device(sizes, tokens, proj_in, proj_out, expert_up, expert_down, expert_ids, weight_codes):
    groups = sizes["grp"]
    blocks = groups
    rows = tokens.shape[0] // blocks
    picks = expert_ids.shape[1]
    experts = sizes["ep"] * groups
    hits = rows * (picks // 2) // groups
    cap = max(2, (4 * rows * picks + 3 * experts - 1) // (3 * experts))
    latent, features = proj_in.shape[0] * sizes["ep"], proj_in.shape[1]
    hidden = expert_up.shape[2]
    quarter, half = latent // 4, latent // 2
    chunks = 4 * blocks
    pieces, split = 2, 4
    wide = latent // split
    vm = pltpu.VMEM
    dma = pltpu.SemaphoreType.DMA
    scratch = [
        vm((latent, hidden), BF), vm((hidden, latent), BF),
        vm((3, *proj_in.shape), BF), vm((4, *proj_out.shape), BF),
        vm((4, blocks, 8, hits), F32), vm((blocks, rows, hits), BF), vm((blocks, hits, rows), BF),
        vm((blocks, rows, rows), F32),
        vm((blocks, 4, cap, hits), BF), vm((blocks, 4, hits, cap), BF),
        vm((chunks, rows, quarter), F32),
        *[vm((chunks, rows, quarter), BF)] * 4,
        vm((blocks, 2, rows, half), BF),
        vm((blocks, 4, 2, hits, half), BF),
        vm((4 * cap, latent), BF), vm((4 * cap, hidden), BF),
        vm((blocks, 2, 4, hits, half), BF),
        vm((blocks, 2, 2, hits, half), BF), vm((blocks, 2, 2, hits, half), BF),
        vm((blocks, 2, hits, half), BF),
        *[vm((blocks, split, rows, wide), BF)] * 5,
        vm((blocks, rows, latent), BF),
        dma((2,)), *[dma((4 * pieces + 1,))] * 2, *[dma((5,))] * 2, *[dma((3,))] * 2,
        *[dma((chunks,))] * 4,
        *[dma((2 * blocks, 3))] * 2,
        *[dma((blocks, 2))] * 4,
        *[dma((blocks, split))] * 4,
    ]
    vmem = pl.BlockSpec(memory_space=pltpu.VMEM)
    hbm = pl.BlockSpec(memory_space=pl.ANY)
    return pl.pallas_call(
        functools.partial(fused_kernel, blocks, hits, cap),
        out_shape=jax.ShapeDtypeStruct((tokens.shape[0], features), BF),
        in_specs=[vm_spec for vm_spec in [vmem] * 5] + [hbm, hbm],
        out_specs=vmem,
        scratch_shapes=scratch,
        compiler_params=pltpu.CompilerParams(
            collective_id=0, has_side_effects=True, vmem_limit_bytes=60 << 20
        ),
    )(tokens, expert_ids, weight_codes, proj_in, proj_out, expert_up, expert_down)


def solution(mesh):
    sizes = dict(mesh.shape)
    body = per_device
    if sizes["ep"] == 4 and sizes["grp"] == 4 and sizes["rep"] == 2:
        body = functools.partial(fused_device, sizes)
    in_specs = (
        P(("rep", "ep"), "grp"),
        P("ep", "grp"),
        P("ep", "grp"),
        P(("ep", "grp"), None, None),
        P(("ep", "grp"), None, None),
        P(("rep", "ep"), None),
        P(("rep", "ep"), None),
    )
    out_specs = P(("rep", "ep"), "grp")
    return jax.shard_map(
        body, mesh=mesh, in_specs=in_specs, out_specs=out_specs, check_vma=False
    )
```

time: 121 us -> 92.7 us (0.77)
  Pallas kernels: 117 us -> 86.9 us
  local copies, waits for them, and re-layouts: 2.26 us -> 5.42 us
  other arithmetic: 1.36 us -> 0 us
    pallas_call x1, Pallas kernels: 117 us -> 86.9 us  [fused_device(): pl.pallas_call(functools.partial(fused_kernel, blocks, hits, cap), out_sh...]
    unnamed x1 -> x3, local copies, waits for them, and re-layouts: 2.26 us -> 5.42 us
    concatenate x1 -> x0, other arithmetic: 1.36 us -> none  [fused_device(): routing = jnp.concatenate([expert_ids.T, weight_codes.T], axis=0)]
where the time goes in v1:
time: 92.7 us; the launch traced here: 92.3 us
  Pallas kernels  86.9 us (94%)
  local copies, waits for them, and re-layouts  5.42 us (6%)
    pallas_call x1, Pallas kernels, fused_device(): pl.pallas_call(functools.partial(fused_kernel, blocks, hits, cap), out_sh...  86.9 us
    unnamed x3, local copies, waits for them, and re-layouts  5.42 us

profile of v1, /device:TPU:0, one launch (start us, length us, event | category | flops | bytes accessed | tf_op | source)
XLA Modules:
  0.0 92.3 jit_solution(14633227341807107558)
XLA Ops:
  0.0 1.6 %copy.8.ids = s32[512,6]{1,0:T(8,128)} copy(s32[512,6]{0,1:T(8,128)} %param.12) | data formatting | bytes 24576 | tf_op args[5]
  1.6 1.6 %copy.9.codes = s32[512,6]{1,0:T(8,128)} copy(s32[512,6]{0,1:T(8,128)} %param.13) | data formatting | bytes 24576 | tf_op args[6]
  3.2 86.9 %shard_map.73 = bf16[512,1024]{1,0:T(8,128)(2,1)} custom-call(bf16[512,1024]{1,0:T(8,128)(2,1)} %tok.1, s32[512,6]{1,0:T(8,128)} %copy.8.ids, s32[512,6]{1,0:T(8,128)} %copy.9.codes, bf16[256,1024]{1,0:T(8,128)(2,1)} %pin.1, bf16[256,1024]{1,0:T(8,128)(2,1)} %pout.1, bf16[1,1024,2688]{2,1,0:T(8,128)(2,1)} %up_hbm.1, bf16[1,2688,1024]{2,1,0:T(8,128)(2,1)} %down_hbm.1), custom_call_target="tpu_custom_call" | custom-call | tf_op jit(solution)/shard_map/pallas_call | solution.py:557
  90.1 2.3 %copy.11 = bf16[512,1024]{1,0:T(8,128)(2,1)} copy(bf16[512,1024]{1,0:T(8,128)(2,1)} %shard_map.73) | data formatting | bytes 2097152

commit v2 on v1

--- a/solution.py
+++ b/solution.py
@@ -86,38 +86,50 @@
 
 SHARED = ("E1", "E2", "E3", "META", "O", "P", "Q")
 OUTER = (
-    ("P", 0), ("META",), ("P", 1), ("GWX", 0), ("WOUT",), ("GWX", 1), ("METAR",), ("T", 0), ("GWM", 0),
-    ("Q", 0), ("Q", 1), ("T", 1), ("Q", 2), ("Q", 3), ("T", 2), ("GWM", 1), ("P", 2), ("P", 3), ("T", 3),
-    ("WX",), ("T", 4), ("D", 0, 0), ("T", 5), ("D", 1, 0), ("T", 6), ("D", 2, 0), ("R", 0, 0), ("T", 7),
-    ("D", 3, 0), ("WR",), ("R", 1, 0), ("T", 8), ("T", 9), ("R", 2, 0), ("T", 10), ("D", 0, 1), ("R", 3, 0),
-    ("T", 11), ("D", 1, 1), ("T", 12), ("R", 0, 1), ("T", 13), ("D", 2, 1), ("E1", 0), ("T", 14), ("R", 1,
-    1), ("E2", 0), ("E3", 0, 0), ("T", 15), ("D", 3, 1), ("R", 2, 1), ("E3", 0, 1), ("M", 0, 0), ("E1", 1),
-    ("M", 0, 1), ("E2", 1), ("R", 3, 1), ("E3", 1, 0), ("E3", 1, 1), ("Y", 0, 0), ("M", 1, 0), ("E1", 2),
-    ("M", 1, 1), ("Y", 0, 1), ("E2", 2), ("E3", 2, 0), ("Y", 1, 0), ("E3", 2, 1), ("M", 2, 0), ("Y", 1, 1),
-    ("E1", 3), ("M", 2, 1), ("E2", 3), ("H", 0, 0), ("E3", 3, 0), ("H", 0, 1), ("Y", 2, 0), ("E3", 3, 1),
-    ("H", 0, 2), ("M", 3, 0), ("Y", 2, 1), ("M", 3, 1), ("H", 0, 3), ("O", 0), ("H", 1, 0), ("Y", 3, 0),
-    ("H", 1, 1), ("Y", 3, 1), ("H", 1, 2), ("H", 1, 3), ("O", 1), ("H", 2, 0), ("H", 2, 1), ("H", 2, 2),
-    ("H", 2, 3), ("O", 2), ("H", 3, 0), ("H", 3, 1), ("H", 3, 2), ("H", 3, 3), ("O", 3),
+    ("P", 0), ("META",), ("P", 1), ("GWX", 0), ("WOUT",), ("GWX", 1), ("GWX", 2), ("GWM", 0), ("GWX", 3),
+    ("METAR",), ("GWM", 1), ("Q", 0), ("Q", 1), ("GWM", 2), ("Q", 2), ("T", 0), ("GWM", 3), ("D", 0, 0),
+    ("Q", 3), ("P", 2), ("T", 1), ("D", 1, 0), ("P", 3), ("WX",), ("T", 2), ("D", 2, 0), ("R", 0, 0), ("T",
+    3), ("D", 3, 0), ("R", 1, 0), ("T", 4), ("D", 0, 1), ("R", 2, 0), ("T", 5), ("D", 1, 1), ("R", 3, 0),
+    ("T", 6), ("D", 2, 1), ("R", 0, 1), ("T", 7), ("D", 3, 1), ("WR",), ("R", 1, 1), ("R", 2, 1), ("T", 8),
+    ("D", 0, 2), ("R", 3, 1), ("T", 9), ("D", 0, 3), ("T", 10), ("D", 1, 2), ("R", 0, 2), ("T", 11), ("D",
+    1, 3), ("R", 0, 3), ("T", 12), ("D", 2, 2), ("E1", 0), ("R", 1, 2), ("T", 13), ("D", 2, 3), ("E2", 0),
+    ("R", 1, 3), ("E3", 0, 0), ("T", 14), ("D", 3, 2), ("E3", 0, 1), ("R", 2, 2), ("E3", 0, 2), ("M", 0, 0),
+    ("T", 15), ("D", 3, 3), ("M", 0, 1), ("E3", 0, 3), ("R", 2, 3), ("M", 0, 2), ("E1", 1), ("M", 0, 3),
+    ("E2", 1), ("R", 3, 2), ("E3", 1, 0), ("Y", 0, 0), ("E3", 1, 1), ("E3", 1, 2), ("R", 3, 3), ("M", 1, 0),
+    ("E3", 1, 3), ("M", 1, 1), ("E1", 2), ("M", 1, 2), ("Y", 0, 1), ("M", 1, 3), ("E2", 2), ("Y", 0, 2),
+    ("E3", 2, 0), ("Y", 0, 3), ("E3", 2, 1), ("E3", 2, 2), ("M", 2, 0), ("Y", 1, 0), ("E3", 2, 3), ("M", 2,
+    1), ("Y", 1, 1), ("E1", 3), ("M", 2, 2), ("M", 2, 3), ("Y", 1, 2), ("E2", 3), ("Y", 1, 3), ("E3", 3, 0),
+    ("E3", 3, 1), ("Y", 2, 0), ("E3", 3, 2), ("M", 3, 0), ("E3", 3, 3), ("M", 3, 1), ("Y", 2, 1), ("M", 3,
+    2), ("Y", 2, 2), ("M", 3, 3), ("H", 0, 0), ("Y", 2, 3), ("Y", 3, 0), ("H", 0, 1), ("Y", 3, 1), ("Y", 3,
+    2), ("H", 0, 2), ("Y", 3, 3), ("H", 0, 3), ("O", 0), ("H", 1, 0), ("H", 1, 1), ("H", 1, 2), ("H", 1, 3),
+    ("O", 1), ("H", 2, 0), ("H", 2, 1), ("H", 2, 2), ("H", 2, 3), ("O", 2), ("H", 3, 0), ("H", 3, 1), ("H",
+    3, 2), ("H", 3, 3), ("O", 3),
 )
 INNER = (
-    ("P", 0), ("META",), ("P", 1), ("F1", 0), ("GWX", 0), ("F1", 1), ("WOUT",), ("F2", 0), ("F1", 2), ("F2",
-    1), ("GWX", 1), ("F1", 3), ("METAR",), ("GWM", 0), ("F2", 2), ("F1", 4), ("Q", 0), ("Q", 1), ("F2", 3),
-    ("F1", 5), ("Q", 2), ("Q", 3), ("GWM", 1), ("F1", 6), ("F2", 4), ("D", 0, 0), ("P", 2), ("P", 3), ("F1",
-    7), ("F2", 5), ("D", 1, 0), ("WX",), ("F2", 6), ("F1", 8), ("D", 2, 0), ("R", 0, 0), ("F1", 9), ("F2",
-    7), ("D", 3, 0), ("F1", 10), ("F2", 8), ("R", 1, 0), ("F1", 11), ("F2", 9), ("R", 2, 0), ("F1", 12),
-    ("F2", 10), ("D", 0, 1), ("WR",), ("F1", 13), ("F2", 11), ("D", 1, 1), ("R", 3, 0), ("F1", 14), ("F2",
-    12), ("R", 0, 1), ("F1", 15), ("F2", 13), ("D", 2, 1), ("E1", 0), ("F2", 14), ("R", 1, 1), ("E2", 0),
-    ("F2", 15), ("D", 3, 1), ("E3", 0, 0), ("R", 2, 1), ("E3", 0, 1), ("E1", 1), ("R", 3, 1), ("M", 0, 0),
-    ("M", 0, 1), ("E2", 1), ("E3", 1, 0), ("E3", 1, 1), ("Y", 0, 0), ("M", 1, 0), ("E1", 2), ("M", 1, 1),
-    ("Y", 0, 1), ("E2", 2), ("E3", 2, 0), ("Y", 1, 0), ("E3", 2, 1), ("G1", 0, 0), ("M", 2, 0), ("Y", 1, 1),
-    ("G1", 0, 1), ("E1", 3), ("G1", 0, 2), ("M", 2, 1), ("G2", 0, 0), ("E2", 3), ("G1", 0, 3), ("Y", 2, 0),
-    ("G2", 0, 1), ("E3", 3, 0), ("G1", 1, 0), ("G2", 0, 2), ("Y", 2, 1), ("G1", 1, 1), ("E3", 3, 1), ("G1",
-    1, 2), ("G2", 0, 3), ("M", 3, 0), ("G2", 1, 0), ("O", 0), ("G1", 1, 3), ("M", 3, 1), ("G2", 1, 1),
-    ("G1", 2, 0), ("G2", 1, 2), ("Y", 3, 0), ("G1", 2, 1), ("G2", 1, 3), ("O", 1), ("G1", 2, 2), ("Y", 3,
-    1), ("G2", 2, 0), ("G1", 2, 3), ("G2", 2, 1), ("G1", 3, 0), ("G2", 2, 2), ("G1", 3, 1), ("G2", 2, 3),
-    ("O", 2), ("G1", 3, 2), ("G2", 3, 0), ("G1", 3, 3), ("G2", 3, 1), ("G2", 3, 2), ("G2", 3, 3), ("O", 3),
+    ("P", 0), ("META",), ("P", 1), ("GWX", 0), ("F1", 0), ("WOUT",), ("GWX", 1), ("F1", 1), ("GWX", 2),
+    ("F1", 2), ("GWM", 0), ("F2", 0), ("D", 0, 0), ("GWX", 3), ("F1", 3), ("METAR",), ("GWM", 1), ("F2", 1),
+    ("D", 1, 0), ("F1", 4), ("Q", 0), ("GWM", 2), ("F2", 2), ("D", 2, 0), ("F1", 5), ("Q", 1), ("GWM", 3),
+    ("F2", 3), ("D", 3, 0), ("F1", 6), ("Q", 2), ("Q", 3), ("F1", 7), ("F2", 4), ("D", 0, 1), ("WX",), ("P",
+    2), ("F2", 5), ("D", 1, 1), ("R", 0, 0), ("P", 3), ("R", 1, 0), ("F2", 6), ("D", 2, 1), ("R", 2, 0),
+    ("F1", 8), ("F2", 7), ("D", 3, 1), ("R", 3, 0), ("F1", 9), ("R", 0, 1), ("R", 1, 1), ("F1", 10), ("R",
+    2, 1), ("F2", 8), ("D", 0, 2), ("F1", 11), ("R", 3, 1), ("WR",), ("F2", 9), ("D", 0, 3), ("F1", 12),
+    ("F2", 10), ("D", 1, 2), ("F1", 13), ("R", 0, 2), ("F2", 11), ("D", 1, 3), ("F1", 14), ("R", 0, 3),
+    ("F2", 12), ("D", 2, 2), ("F1", 15), ("E1", 0), ("R", 1, 2), ("F2", 13), ("D", 2, 3), ("E2", 0), ("R",
+    1, 3), ("E3", 0, 0), ("F2", 14), ("D", 3, 2), ("E3", 0, 1), ("R", 2, 2), ("E3", 0, 2), ("F2", 15), ("D",
+    3, 3), ("M", 0, 0), ("M", 0, 1), ("E3", 0, 3), ("R", 2, 3), ("M", 0, 2), ("E1", 1), ("M", 0, 3), ("E2",
+    1), ("R", 3, 2), ("E3", 1, 0), ("E3", 1, 1), ("R", 3, 3), ("E3", 1, 2), ("M", 1, 0), ("Y", 0, 0), ("E3",
+    1, 3), ("M", 1, 1), ("M", 1, 2), ("Y", 0, 1), ("E1", 2), ("M", 1, 3), ("Y", 0, 2), ("E2", 2), ("Y", 0,
+    3), ("E3", 2, 0), ("E3", 2, 1), ("Y", 1, 0), ("E3", 2, 2), ("M", 2, 0), ("E3", 2, 3), ("M", 2, 1), ("Y",
+    1, 1), ("E1", 3), ("M", 2, 2), ("M", 2, 3), ("Y", 1, 2), ("G1", 0, 0), ("E2", 3), ("Y", 1, 3), ("E3", 3,
+    0), ("E3", 3, 1), ("Y", 2, 0), ("E3", 3, 2), ("M", 3, 0), ("G1", 0, 1), ("Y", 2, 1), ("M", 3, 1), ("E3",
+    3, 3), ("M", 3, 2), ("Y", 2, 2), ("G2", 0, 0), ("G1", 0, 2), ("M", 3, 3), ("Y", 2, 3), ("G1", 0, 3),
+    ("Y", 3, 0), ("G2", 0, 1), ("G1", 1, 0), ("Y", 3, 1), ("G2", 0, 2), ("G1", 1, 1), ("Y", 3, 2), ("Y", 3,
+    3), ("G2", 0, 3), ("G1", 1, 2), ("O", 0), ("G2", 1, 0), ("G1", 1, 3), ("G2", 1, 1), ("G1", 2, 0), ("G2",
+    1, 2), ("G1", 2, 1), ("G2", 1, 3), ("G1", 2, 2), ("O", 1), ("G2", 2, 0), ("G1", 2, 3), ("G2", 2, 1),
+    ("G1", 3, 0), ("G2", 2, 2), ("G1", 3, 1), ("G2", 2, 3), ("G1", 3, 2), ("O", 2), ("G2", 3, 0), ("G1", 3,
+    3), ("G2", 3, 1), ("G2", 3, 2), ("G2", 3, 3), ("O", 3),
 )
-CHUNKS = ((0, 0), (0, 1), (0, 2), (0, 3), (1, 0), (1, 1), (1, 2), (1, 3), (2, 0), (2, 1), (3, 0), (3, 1), (2, 2), (3, 2), (2, 3), (3, 3))
+CHUNKS = ((0, 0), (0, 1), (0, 2), (0, 3), (1, 0), (1, 1), (1, 2), (1, 3), (2, 0), (3, 0), (2, 1), (3, 1), (2, 2), (3, 2), (2, 3), (3, 3))
 
 
 def segments():
@@ -143,8 +155,7 @@
 ):
     rep, ep, z = lax.axis_index("rep"), lax.axis_index("ep"), lax.axis_index("grp")
     chip = ep // 2
-    side = ep % 2
-    mate = chip * 2 + (1 - side)
+    mate = chip * 2 + (1 - ep % 2)
     ypart = (ep + 2) % 4
     inward = jnp.where(z < 2, z + 1, z - 1)
     outward = jnp.where(z < 2, jnp.maximum(z - 1, 0), jnp.minimum(z + 1, 3))
@@ -152,10 +163,8 @@
     outer = jnp.logical_not(inner)
     rows = tok.shape[0] // blocks
     quarter = pin.shape[0]
-    half = 2 * quarter
-    picks = ids.shape[1]
+    picks = ids.shape[0]
     pieces = ws.shape[0] // 4
-    prow = quarter // 2 // pieces
     split = sown.shape[1]
     width = sown.shape[3]
 
@@ -227,7 +236,7 @@
         if q < 2:
             ready = [(q, b) for b in range(blocks)]
         else:
-            ready = CHUNKS[2 * blocks :][:2] if q == 2 else CHUNKS[2 * blocks + 2 :]
+            ready = CHUNKS[2 * blocks :][:1] if q == 2 else CHUNKS[2 * blocks + 1 :]
 
         @pl.when(outer)
         def _():
@@ -246,9 +255,12 @@
         copy.start()
     send_own(0)
 
+    across_mate = (ypart // 2) * 2 + 1 - ypart % 2
+    shards = (ep, mate, ypart, across_mate)
+    arriving = (ypart, across_mate, ep, mate)
+
     def put(q, b, v):
-        column = pl.multiple_of(jnp.where(q % 2 == 0, side, 1 - side) * quarter, quarter)
-        lat[b, jnp.where(q < 2, chip, 1 - chip), :, pl.ds(column, quarter)] = v.astype(BF)
+        lat[b, shards[q]] = v.astype(BF)
 
     def op_f1(k):
         from_outer(k).wait_recv()
@@ -278,13 +290,9 @@
         return jnp.where(jnp.logical_and(slot == rank, sel > 0.0), 1.0, 0.0)
 
     def op_meta():
-        i = lax.broadcasted_iota(jnp.int32, (8, picks), 0)
-        j = lax.broadcasted_iota(jnp.int32, (8, picks), 1)
-        pickrow = jnp.where(i == j, 1.0, 0.0).astype(BF)
-        id_rows = nt(pickrow, ids[...].astype(F32).astype(BF))
-        code_rows = nt(pickrow, codes[...].astype(F32).astype(BF))
+        id_rows, code_rows = ids[...], codes[...].astype(F32)
         n = id_rows.shape[1]
-        here = (lax.broadcasted_iota(jnp.int32, (8, n), 0) * blocks + z).astype(F32)
+        here = lax.broadcasted_iota(jnp.int32, (8, n), 0) * blocks + z
         table = jnp.zeros((8, n), F32)
         for p in range(picks):
             table = table + jnp.where(id_rows[p : p + 1, :] == here, code_rows[p : p + 1, :], 0.0)
@@ -318,31 +326,29 @@
             pick[b, s] = q.astype(BF)
             scale[b, s] = jnp.transpose(q * m).astype(BF)
 
-    def x_copies(b, g):
-        mine = jnp.where(g == 0, chip, 1 - chip)
-        other = 1 - mine
-        k = 2 * b + g
+    def x_copies(b, q):
+        mine, other = shards[q], arriving[q]
+        k = 4 * b + q
         return (
             rcopy(xs.at[b, 0, mine], xs.at[b, 1, mine], xss.at[k, 0], xsr.at[k, 0], ep=ypart),
             rcopy(xs.at[b, 0, mine], xs.at[b, 2, mine], xss.at[k, 1], xsr.at[k, 1], ep=mate),
             rcopy(xs.at[b, 1, other], xs.at[b, 3, other], xss.at[k, 2], xsr.at[k, 2], ep=mate),
         )
 
-    def op_d(b, g):
-        mine = jnp.where(g == 0, chip, 1 - chip)
-        xs[b, 0, mine] = nn(onehot[b], lat[b, mine]).astype(BF)
-        to_y, to_m, _ = x_copies(b, g)
+    def op_d(b, q):
+        xs[b, 0, shards[q]] = nn(onehot[b], lat[b, shards[q]]).astype(BF)
+        to_y, to_m, _ = x_copies(b, q)
         to_y.start()
         to_m.start()
 
-    def op_r(b, g):
-        to_y, _, relay = x_copies(b, g)
+    def op_r(b, q):
+        to_y, _, relay = x_copies(b, q)
         to_y.wait_recv()
         relay.start()
 
     def op_w(b):
-        for g in range(2):
-            _, to_m, relay = x_copies(b, g)
+        for q in range(4):
+            _, to_m, relay = x_copies(b, q)
             to_m.wait_recv()
             relay.wait_recv()
 
@@ -358,9 +364,9 @@
             for load in loads:
                 load.wait()
         for s in range(4):
-            for h in range(2):
-                xin[s * cap : (s + 1) * cap, h * half : (h + 1) * half] = nn(
-                    pick[b, s], xs[b, s, h]
+            for q in range(4):
+                xin[s * cap : (s + 1) * cap, q * quarter : (q + 1) * quarter] = nn(
+                    pick[b, s], xs[b, s, q]
                 ).astype(BF)
         raised(slice(0, cut))
 
@@ -374,7 +380,7 @@
         return rcopy(zsum.at[b, h, 1], yret.at[b, h], yss.at[b, h], ysr.at[b, h], ep=ypart)
 
     def op_e3(b, h):
-        o = nn(hid[...], down[:, h * half : (h + 1) * half]).astype(BF)
+        o = nn(hid[...], down[:, h * width : (h + 1) * width]).astype(BF)
         for s in (2, 3, 0, 1):
             ys[b, h, s] = nn(scale[b, s], o[s * cap : (s + 1) * cap, :]).astype(BF)
         m_copy(b, h).start()
@@ -393,19 +399,14 @@
     def to_outer2(b, c):
         return rcopy(s4.at[b, c], f4.at[b, c], co.at[b, c], rd.at[b, c], grp=outward)
 
-    per_half = split // 2
-
-    def op_y(b, h):
-        y_copy(b, h).wait_recv()
-        v = (zsum[b, h, 0].astype(F32) + yret[b, h].astype(F32)).astype(BF)
-        v = nn(onehot_t[b], v).astype(BF)
-        for i in range(per_half):
-            sown[b, h * per_half + i] = v[:, i * width : (i + 1) * width]
+    def op_y(b, c):
+        y_copy(b, c).wait_recv()
+        v = (zsum[b, c, 0].astype(F32) + yret[b, c].astype(F32)).astype(BF)
+        sown[b, c] = nn(onehot_t[b], v).astype(BF)
 
         @pl.when(outer)
         def _():
-            for i in range(per_half):
-                from_outer2(b, h * per_half + i).start()
+            from_outer2(b, c).start()
 
     def op_g1(b, c):
         from_outer2(b, c).wait_recv()
@@ -497,12 +498,12 @@
     for k in range(4 * blocks):
         from_outer(k).wait_send()
     for b in range(blocks):
-        for h in range(2):
-            for copy in x_copies(b, h):
+        for q in range(4):
+            for copy in x_copies(b, q):
                 copy.wait_send()
-            m_copy(b, h).wait_send()
-            y_copy(b, h).wait_send()
         for c in range(split):
+            m_copy(b, c).wait_send()
+            y_copy(b, c).wait_send()
             from_outer2(b, c).wait_send()
 
     @pl.when(inner)
@@ -524,9 +525,9 @@
     cap = max(2, (4 * rows * picks + 3 * experts - 1) // (3 * experts))
     latent, features = proj_in.shape[0] * sizes["ep"], proj_in.shape[1]
     hidden = expert_up.shape[2]
-    quarter, half = latent // 4, latent // 2
+    quarter = latent // 4
     chunks = 4 * blocks
-    pieces, split = 2, 4
+    pieces, split = 4, 4
     wide = latent // split
     vm = pltpu.VMEM
     dma = pltpu.SemaphoreType.DMA
@@ -538,19 +539,18 @@
         vm((blocks, 4, cap, hits), BF), vm((blocks, 4, hits, cap), BF),
         vm((chunks, rows, quarter), F32),
         *[vm((chunks, rows, quarter), BF)] * 4,
-        vm((blocks, 2, rows, half), BF),
-        vm((blocks, 4, 2, hits, half), BF),
+        vm((blocks, 4, rows, quarter), BF),
+        vm((blocks, 4, 4, hits, quarter), BF),
         vm((4 * cap, latent), BF), vm((4 * cap, hidden), BF),
-        vm((blocks, 2, 4, hits, half), BF),
-        vm((blocks, 2, 2, hits, half), BF), vm((blocks, 2, 2, hits, half), BF),
-        vm((blocks, 2, hits, half), BF),
+        vm((blocks, split, 4, hits, wide), BF),
+        vm((blocks, split, 2, hits, wide), BF), vm((blocks, split, 2, hits, wide), BF),
+        vm((blocks, split, hits, wide), BF),
         *[vm((blocks, split, rows, wide), BF)] * 5,
         vm((blocks, rows, latent), BF),
         dma((2,)), *[dma((4 * pieces + 1,))] * 2, *[dma((5,))] * 2, *[dma((3,))] * 2,
         *[dma((chunks,))] * 4,
-        *[dma((2 * blocks, 3))] * 2,
-        *[dma((blocks, 2))] * 4,
-        *[dma((blocks, split))] * 4,
+        *[dma((4 * blocks, 3))] * 2,
+        *[dma((blocks, split))] * 8,
     ]
     vmem = pl.BlockSpec(memory_space=pltpu.VMEM)
     hbm = pl.BlockSpec(memory_space=pl.ANY)
@@ -563,7 +563,7 @@
         compiler_params=pltpu.CompilerParams(
             collective_id=0, has_side_effects=True, vmem_limit_bytes=60 << 20
         ),
-    )(tokens, expert_ids, weight_codes, proj_in, proj_out, expert_up, expert_down)
+    )(tokens, expert_ids.T, weight_codes.T, proj_in, proj_out, expert_up, expert_down)
 
 
 def solution(mesh):

time: 92.7 us -> 92.5 us (level)
  Pallas kernels: 86.9 us -> 90.1 us
  local copies, waits for them, and re-layouts: 5.42 us -> 2.26 us
    pallas_call x1, Pallas kernels: 86.9 us -> 90.1 us  [fused_device(): pl.pallas_call(functools.partial(fused_kernel, blocks, hits, cap), out_sh...]
    unnamed x3 -> x1, local copies, waits for them, and re-layouts: 5.42 us -> 2.26 us
where the time goes in v2:
time: 92.5 us; the launch traced here: 92.3 us
  Pallas kernels  90.1 us (97%)
  local copies, waits for them, and re-layouts  2.26 us (2%)
    pallas_call x1, Pallas kernels, fused_device(): pl.pallas_call(functools.partial(fused_kernel, blocks, hits, cap), out_sh...  90.1 us
    unnamed x1, local copies, waits for them, and re-layouts  2.26 us

profile of v2, /device:TPU:0, one launch (start us, length us, event | category | flops | bytes accessed | tf_op | source)
XLA Modules:
  0.0 92.3 jit_solution(2616076631264560517)
XLA Ops:
  0.0 90.1 %shard_map.73 = bf16[512,1024]{1,0:T(8,128)(2,1)} custom-call(bf16[512,1024]{1,0:T(8,128)(2,1)} %tok.1, s32[6,512]{1,0:T(8,128)} %bitcast.2, s32[6,512]{1,0:T(8,128)} %bitcast.3, bf16[256,1024]{1,0:T(8,128)(2,1)} %pin.1, bf16[256,1024]{1,0:T(8,128)(2,1)} %pout.1, bf16[1,1024,2688]{2,1,0:T(8,128)(2,1)} %up_hbm.1, bf16[1,2688,1024]{2,1,0:T(8,128)(2,1)} %down_hbm.1), custom_call_target="tpu_custom_call" | custom-call | tf_op jit(solution)/shard_map/pallas_call | solution.py:557
  90.1 2.3 %copy.9 = bf16[512,1024]{1,0:T(8,128)(2,1)} copy(bf16[512,1024]{1,0:T(8,128)(2,1)} %shard_map.73) | data formatting | bytes 2097152
